TPU v7x, 512 devices: a whole 4x8x8 slice. The times are simulated.
512 devices in a mesh: band: 8 (over z_lo, core), dom: 64 (over x, y, z_hi).
Axes of the slice: x: 4, y: 8, z: 8 (z_hi: 2, z_lo: 4; z = z_hi * 4 + z_lo), core: 2. Of those that a mesh axis runs over, the one named last changes fastest.
Arguments:
- orbitals: float32 [96, 128, 128, 128], P('band', 'dom'), may hold values from -6 to 6
- occupations: float32 [96], replicated, may hold values from 0.25 to 2
Outputs:
- exchange_terms: float32 [96, 128, 128, 128], P('band', 'dom')
All inputs are finite; a program needn't handle non-finite values.
Results may differ from a plain program's by a relative error of at most 0.0001.
Values sent between devices are 32-bit elements; how exact they have to be, the bound alone decides.
A program may use at most 128 MiB of HBM per device.

v0:
```python
import jax
import jax.numpy as jnp
from jax import lax
from jax.sharding import PartitionSpec as P

BLOCK = 2
STEPS = 2
SWEEPS = 2


def from_root(block, axis, source):
    block = jnp.where(lax.axis_index(axis) == source, block, jnp.zeros_like(block))
    return lax.psum(block, axis)


def extended(cells, sides, width):
    for axis, dim in sides:
        count = lax.axis_size(axis)
        ends = count - 1
        head = lax.slice_in_dim(cells, 0, width, axis=dim)
        tail = lax.slice_in_dim(cells, cells.shape[dim] - width, cells.shape[dim], axis=dim)
        cells = jnp.concatenate(
            [
                lax.ppermute(tail, axis, [(i, (i + 1) % count) for i in range(ends)]),
                cells,
                lax.ppermute(head, axis, [((i + 1) % count, i) for i in range(ends)]),
            ],
            axis=dim,
        )
    return cells


def lateral(field):
    padded = jnp.pad(field, ((0, 0), (0, 0), (1, 1), (1, 1)))
    total = padded[:, :, 2:, 1:-1] + padded[:, :, :-2, 1:-1]
    return total + padded[:, :, 1:-1, 2:] + padded[:, :, 1:-1, :-2]


def per_device(orbitals, occupations):
    orb_count, planes, cells_y, cells_z = orbitals.shape
    groups = lax.axis_size("band")
    exchange_terms = jnp.zeros(orbitals.shape, jnp.float32)
    for step_index in range(STEPS):
        owner = step_index * (groups // STEPS)
        first = owner * orb_count + step_index * BLOCK
        mine = orbitals[step_index * BLOCK : (step_index + 1) * BLOCK]
        owner_block = from_root(mine, "band", owner)
        weights = occupations[first : first + BLOCK]
        density = (owner_block[:, None] * orbitals[None]).reshape(
            BLOCK * orb_count, planes, cells_y, cells_z
        )
        potential = density / 6.0
        for sweep_index in range(SWEEPS):
            padded = extended(potential, (("dom", 1),), 1)
            along_x = padded[:, 2:] + padded[:, :-2]
            potential = (density + along_x + lateral(potential)) / 6.0
        potential = potential.reshape(BLOCK, orb_count, planes, cells_y, cells_z)
        step_sum = jnp.zeros(orbitals.shape, jnp.float32)
        for block_index in range(BLOCK):
            step_sum = (
                step_sum
                - weights[block_index] * potential[block_index] * owner_block[block_index][None]
            )
        exchange_terms = exchange_terms + step_sum
    return exchange_terms


def solution(mesh):
    in_specs = (P("band", "dom", None, None), P())
    out_specs = P("band", "dom", None, None)
    return jax.shard_map(
        per_device, mesh=mesh, in_specs=in_specs, out_specs=out_specs, check_vma=False
    )
```

profile of v0, /device:TPU:58, one launch (start us, length us, event | category | flops | bytes accessed | tf_op | source)
XLA Modules:
  0.0 701.8 jit_solution(2163669091845171752)
XLA Ops:
  6.5 1.8 slice_select_fusion.1
  8.4 0.0 all-reduce.7.cloned.1.call-update
  8.4 83.7 %all-reduce.7.cloned.1.call-done = (f32[2,2,128,128]{3,2,1,0:T(8,128)}, f32[2,2,128,128]{3,2,1,0:T(8,128)}) async-done(((f32[2,2,128,128]{3,2,1,0:T(8,128)}, f32[2,2,128,128]{3,2,1,0:T(8,128)}), (f32[2,2,128,128]{3,2,1,0:T(8,128)}, f32[2,2,128,128]{3,2,1,0:T(8,128)})) %all-reduce.7.cloned.1.call-update) | async-done | bytes 524304 | tf_op jit(solution)/shard_map/psum | solution.py:13
  92.1 2.3 broadcast_multiply_fusion.1
  94.3 1.2 bitcast_multiply_fusion
  95.6 0.3 fusion.38
  96.0 6.4 collective-permute-start
  102.3 3.4 collective-permute-start.1
  105.7 0.3 fusion.40
  106.1 7.3 %collective-permute-start.4 = (f32[24,1,128,128]{3,2,1,0:T(8,128)S(1)}, f32[24,1,128,128]{3,2,1,0:T(8,128)S(1)}, u32[]{:S(2)}, u32[]{:S(2)}) collective-permute-start(f32[24,1,128,128]{3,2,1,0:T(8,128)S(1)} %get-tuple-element.13), channel_id=1, source_target_pairs={{1,0},{2,1},{3,2},{4,3},{5,4},{6,5},{7,6},{8,7},{9,8},{10,9},{11,1... | collective-permute-start | bytes 4718600 | tf_op jit(solution)/shard_map/ppermute | solution.py:26
  113.3 3.2 collective-permute-start.5
  116.5 215.8 %collective-permute-done = f32[24,1,128,128]{3,2,1,0:T(8,128)S(1)} collective-permute-done((f32[24,1,128,128]{3,2,1,0:T(8,128)S(1)}, f32[24,1,128,128]{3,2,1,0:T(8,128)S(1)}, u32[]{:S(2)}, u32[]{:S(2)}) %collective-permute-start) | collective-permute-done | bytes 1572896 | tf_op jit(solution)/shard_map/ppermute | solution.py:26
  332.3 175.8 %collective-permute-done.1 = f32[24,1,128,128]{3,2,1,0:T(8,128)S(1)} collective-permute-done((f32[24,1,128,128]{3,2,1,0:T(8,128)S(1)}, f32[24,1,128,128]{3,2,1,0:T(8,128)S(1)}, u32[]{:S(2)}, u32[]{:S(2)}) %collective-permute-start.1) | collective-permute-done | bytes 1572896 | tf_op jit(solution)/shard_map/ppermute | solution.py:24
  508.1 2.2 fusion.4
  510.3 0.3 fusion.37
  510.7 1.9 collective-permute-start.2
  512.6 8.4 %collective-permute-start.3 = (f32[24,1,128,128]{3,2,1,0:T(8,128)S(1)}, f32[24,1,128,128]{3,2,1,0:T(8,128)S(1)}, u32[]{:S(2)}, u32[]{:S(2)}) collective-permute-start(f32[24,1,128,128]{3,2,1,0:T(8,128)S(1)} %get-tuple-element.8), channel_id=1, source_target_pairs={{0,1},{1,2},{2,3},{3,4},{4,5},{5,6},{6,7},{7,8},{8,9},{9,10},{10,1... | collective-permute-start | bytes 4718600 | tf_op jit(solution)/shard_map/ppermute | solution.py:24
  521.0 0.0 collective-permute-done.4
  521.0 82.3 %collective-permute-done.5 = f32[24,1,128,128]{3,2,1,0:T(8,128)S(1)} collective-permute-done((f32[24,1,128,128]{3,2,1,0:T(8,128)S(1)}, f32[24,1,128,128]{3,2,1,0:T(8,128)S(1)}, u32[]{:S(2)}, u32[]{:S(2)}) %collective-permute-start.5) | collective-permute-done | bytes 1572896 | tf_op jit(solution)/shard_map/ppermute | solution.py:24
  603.3 2.2 fusion.14
  605.5 0.0 copy-start.2
  605.5 0.3 fusion.39
  605.9 1.9 collective-permute-start.6
  607.8 10.7 %collective-permute-start.7 = (f32[24,1,128,128]{3,2,1,0:T(8,128)S(1)}, f32[24,1,128,128]{3,2,1,0:T(8,128)S(1)}, u32[]{:S(2)}, u32[]{:S(2)}) collective-permute-start(f32[24,1,128,128]{3,2,1,0:T(8,128)S(1)} %get-tuple-element.12), channel_id=1, source_target_pairs={{0,1},{1,2},{2,3},{3,4},{4,5},{5,6},{6,7},{7,8},{8,9},{9,10},{10,1... | collective-permute-start | bytes 4718600 | tf_op jit(solution)/shard_map/ppermute | solution.py:24
  618.5 0.7 fusion.41
  619.2 36.1 %collective-permute-done.2 = f32[24,1,128,128]{3,2,1,0:T(8,128)S(1)} collective-permute-done((f32[24,1,128,128]{3,2,1,0:T(8,128)S(1)}, f32[24,1,128,128]{3,2,1,0:T(8,128)S(1)}, u32[]{:S(2)}, u32[]{:S(2)}) %collective-permute-start.2) | collective-permute-done | bytes 1572896 | tf_op jit(solution)/shard_map/ppermute | solution.py:26
  655.4 0.0 collective-permute-done.3
  655.4 2.2 fusion.9
  657.6 30.7 %collective-permute-done.6 = f32[24,1,128,128]{3,2,1,0:T(8,128)S(1)} collective-permute-done((f32[24,1,128,128]{3,2,1,0:T(8,128)S(1)}, f32[24,1,128,128]{3,2,1,0:T(8,128)S(1)}, u32[]{:S(2)}, u32[]{:S(2)}) %collective-permute-start.6) | collective-permute-done | bytes 1572896 | tf_op jit(solution)/shard_map/ppermute | solution.py:26
  688.3 0.0 collective-permute-done.7
  688.3 2.2 fusion.19
  690.5 4.5 fusion.30
  (7 shorter events, 0.0 us)
Async XLA Ops:
  6.5 85.5 %all-reduce.7.cloned.1.call-start = ((), (), s32[]{:S(2)}) async-start(), calls=%async_computation | async-start | bytes 1048576 | tf_op jit(solution)/shard_map/psum | solution.py:13
  96.0 236.3 %collective-permute-start = (f32[24,1,128,128]{3,2,1,0:T(8,128)S(1)}, f32[24,1,128,128]{3,2,1,0:T(8,128)S(1)}, u32[]{:S(2)}, u32[]{:S(2)}) collective-permute-start(f32[24,1,128,128]{3,2,1,0:T(8,128)S(1)} %get-tuple-element.9), channel_id=1, source_target_pairs={{1,0},{2,1},{3,2},{4,3},{5,4},{6,5},{7,6},{8,7},{9,8},{10,9},{11,1... | collective-permute-start | bytes 4718600 | tf_op jit(solution)/shard_map/ppermute | solution.py:26
  102.3 405.8 %collective-permute-start.1 = (f32[24,1,128,128]{3,2,1,0:T(8,128)S(1)}, f32[24,1,128,128]{3,2,1,0:T(8,128)S(1)}, u32[]{:S(2)}, u32[]{:S(2)}) collective-permute-start(f32[24,1,128,128]{3,2,1,0:T(8,128)S(1)} %get-tuple-element.10), channel_id=1, source_target_pairs={{0,1},{1,2},{2,3},{3,4},{4,5},{5,6},{6,7},{7,8},{8,9},{9,10},{10,1... | collective-permute-start | bytes 4718600 | tf_op jit(solution)/shard_map/ppermute | solution.py:24
  106.1 414.9 %collective-permute-start.4 = (f32[24,1,128,128]{3,2,1,0:T(8,128)S(1)}, f32[24,1,128,128]{3,2,1,0:T(8,128)S(1)}, u32[]{:S(2)}, u32[]{:S(2)}) collective-permute-start(f32[24,1,128,128]{3,2,1,0:T(8,128)S(1)} %get-tuple-element.13), channel_id=1, source_target_pairs={{1,0},{2,1},{3,2},{4,3},{5,4},{6,5},{7,6},{8,7},{9,8},{10,9},{11,1... | collective-permute-start | bytes 4718600 | tf_op jit(solution)/shard_map/ppermute | solution.py:26
  113.3 490.0 %collective-permute-start.5 = (f32[24,1,128,128]{3,2,1,0:T(8,128)S(1)}, f32[24,1,128,128]{3,2,1,0:T(8,128)S(1)}, u32[]{:S(2)}, u32[]{:S(2)}) collective-permute-start(f32[24,1,128,128]{3,2,1,0:T(8,128)S(1)} %get-tuple-element.14), channel_id=1, source_target_pairs={{0,1},{1,2},{2,3},{3,4},{4,5},{5,6},{6,7},{7,8},{8,9},{9,10},{10,1... | collective-permute-start | bytes 4718600 | tf_op jit(solution)/shard_map/ppermute | solution.py:24
  510.7 144.7 %collective-permute-start.2 = (f32[24,1,128,128]{3,2,1,0:T(8,128)S(1)}, f32[24,1,128,128]{3,2,1,0:T(8,128)S(1)}, u32[]{:S(2)}, u32[]{:S(2)}) collective-permute-start(f32[24,1,128,128]{3,2,1,0:T(8,128)S(1)} %get-tuple-element.7), channel_id=1, source_target_pairs={{1,0},{2,1},{3,2},{4,3},{5,4},{6,5},{7,6},{8,7},{9,8},{10,9},{11,1... | collective-permute-start | bytes 4718600 | tf_op jit(solution)/shard_map/ppermute | solution.py:26
  512.6 142.8 %collective-permute-start.3 = (f32[24,1,128,128]{3,2,1,0:T(8,128)S(1)}, f32[24,1,128,128]{3,2,1,0:T(8,128)S(1)}, u32[]{:S(2)}, u32[]{:S(2)}) collective-permute-start(f32[24,1,128,128]{3,2,1,0:T(8,128)S(1)} %get-tuple-element.8), channel_id=1, source_target_pairs={{0,1},{1,2},{2,3},{3,4},{4,5},{5,6},{6,7},{7,8},{8,9},{9,10},{10,1... | collective-permute-start | bytes 4718600 | tf_op jit(solution)/shard_map/ppermute | solution.py:24
  605.5 13.0 %copy-start.2 = (f32[96]{0:T(128)S(1)}, f32[96]{0:T(128)}, u32[]{:S(2)}) copy-start(f32[96]{0:T(128)} %param.3) | copy-start | bytes 1156
  605.5 13.6 %copy-start = (f32[2,2,128,128]{3,2,1,0:T(8,128)S(1)}, f32[2,2,128,128]{3,2,1,0:T(8,128)}, u32[]{:S(2)}) copy-start(f32[2,2,128,128]{3,2,1,0:T(8,128)} %get-tuple-element.5) | copy-start | bytes 786436
  605.5 13.6 %copy-start.1 = (f32[2,2,128,128]{3,2,1,0:T(8,128)S(1)}, f32[2,2,128,128]{3,2,1,0:T(8,128)}, u32[]{:S(2)}) copy-start(f32[2,2,128,128]{3,2,1,0:T(8,128)} %get-tuple-element.6) | copy-start | bytes 786436
  605.9 82.4 %collective-permute-start.6 = (f32[24,1,128,128]{3,2,1,0:T(8,128)S(1)}, f32[24,1,128,128]{3,2,1,0:T(8,128)S(1)}, u32[]{:S(2)}, u32[]{:S(2)}) collective-permute-start(f32[24,1,128,128]{3,2,1,0:T(8,128)S(1)} %get-tuple-element.11), channel_id=1, source_target_pairs={{1,0},{2,1},{3,2},{4,3},{5,4},{6,5},{7,6},{8,7},{9,8},{10,9},{11,1... | collective-permute-start | bytes 4718600 | tf_op jit(solution)/shard_map/ppermute | solution.py:26
  607.8 80.4 %collective-permute-start.7 = (f32[24,1,128,128]{3,2,1,0:T(8,128)S(1)}, f32[24,1,128,128]{3,2,1,0:T(8,128)S(1)}, u32[]{:S(2)}, u32[]{:S(2)}) collective-permute-start(f32[24,1,128,128]{3,2,1,0:T(8,128)S(1)} %get-tuple-element.12), channel_id=1, source_target_pairs={{0,1},{1,2},{2,3},{3,4},{4,5},{5,6},{6,7},{7,8},{8,9},{9,10},{10,1... | collective-permute-start | bytes 4718600 | tf_op jit(solution)/shard_map/ppermute | solution.py:24
Sparse Core Ops, SparseCore 0:
  10.3 81.7 all-reduce.6
where the time goes:
time: 702 us
  waiting for transfers between devices  624 us (89%)
  starting transfers between devices  43 us (6%)
  other arithmetic  18.7 us (3%)
  between operations  13.6 us (2%)
    ppermute x4, waiting for transfers between devices, extended(): lax.ppermute(head, axis, [((i + 1) % count, i) for i in range(ends)])  283 us
    ppermute x4, waiting for transfers between devices, extended(): lax.ppermute(tail, axis, [(i, (i + 1) % count) for i in range(ends)])  258 us
    psum x1, waiting for transfers between devices, from_root(): return lax.psum(block, axis)  83.7 us
    ppermute x4, starting transfers between devices, extended(): lax.ppermute(tail, axis, [(i, (i + 1) % count) for i in range(ends)])  25.6 us
    ppermute x4, starting transfers between devices, extended(): lax.ppermute(head, axis, [((i + 1) % count, i) for i in range(ends)])  17.5 us
  transfers between devices with their start and end apart: 9, of which 6 were waited for; matrix products, arithmetic and copies ran while one was open for 1% of the time, Pallas kernels for 0%

commit v1 on v0

--- a/solution.py
+++ b/solution.py
@@ -10,7 +10,7 @@
 
 def from_root(block, axis, source):
     block = jnp.where(lax.axis_index(axis) == source, block, jnp.zeros_like(block))
-    return lax.psum(block, axis)
+    return jnp.sum(lax.all_gather(block, axis), axis=0)
 
 
 def extended(cells, sides, width):

time: 702 us -> 669 us (0.953)
  the two profiles are of different devices: /device:TPU:58 before, /device:TPU:193 now
where the time goes in v1:
time: 669 us
  waiting for transfers between devices  593 us (89%)
  starting transfers between devices  37.2 us (6%)
  other arithmetic  21 us (3%)
  between operations  13.6 us (2%)
    ppermute x4, waiting for transfers between devices, extended(): lax.ppermute(head, axis, [((i + 1) % count, i) for i in range(ends)])  507 us
    all_gather x2, waiting for transfers between devices, from_root(): return jnp.sum(lax.all_gather(block, axis), axis=0)  85.7 us
    ppermute x4, starting transfers between devices, extended(): lax.ppermute(tail, axis, [(i, (i + 1) % count) for i in range(ends)])  32 us
  transfers between devices with their start and end apart: 10, of which 6 were waited for; matrix products, arithmetic and copies ran while one was open for 2% of the time, Pallas kernels for 0%

profile of v1, /device:TPU:193, one launch (start us, length us, event | category | flops | bytes accessed | tf_op | source)
XLA Modules:
  0.0 668.9 jit_solution(15895826909622044491)
XLA Ops:
  6.5 2.0 slice_select_fusion.1
  8.5 0.0 all-gather.5.cloned.1.call-update
  8.5 0.0 all-gather.7.cloned.1.call-start
  8.6 0.7 all-gather.7.cloned.1.call-update
  9.3 43.8 %all-gather.5.cloned.1.call-done = f32[16,2,128,128]{3,2,1,0:T(8,128)} async-done(((f32[2,2,128,128]{3,2,1,0:T(8,128)}), f32[16,2,128,128]{3,2,1,0:T(8,128)}) %all-gather.5.cloned.1.call-update) | async-done | bytes 2097168 | tf_op jit(solution)/shard_map/all_gather | solution.py:13
  53.1 1.7 reduce_sum.18
  54.9 41.8 %all-gather.7.cloned.1.call-done = f32[16,2,128,128]{3,2,1,0:T(8,128)} async-done(((f32[2,2,128,128]{3,2,1,0:T(8,128)}), f32[16,2,128,128]{3,2,1,0:T(8,128)}) %all-gather.7.cloned.1.call-update) | async-done | bytes 2097168 | tf_op jit(solution)/shard_map/all_gather | solution.py:13
  96.7 1.7 reduce_sum.19
  98.4 1.0 broadcast_multiply_fusion.1
  99.4 1.2 bitcast_multiply_fusion
  100.7 0.3 fusion.38
  101.0 1.3 collective-permute-start
  102.3 8.0 %collective-permute-start.1 = (f32[24,1,128,128]{3,2,1,0:T(8,128)S(1)}, f32[24,1,128,128]{3,2,1,0:T(8,128)S(1)}, u32[]{:S(2)}, u32[]{:S(2)}) collective-permute-start(f32[24,1,128,128]{3,2,1,0:T(8,128)S(1)} %get-tuple-element.8), channel_id=1, source_target_pairs={{0,1},{1,2},{2,3},{3,4},{4,5},{5,6},{6,7},{7,8},{8,9},{9,10},{10,1... | collective-permute-start | bytes 4718600 | tf_op jit(solution)/shard_map/ppermute | solution.py:24
  110.3 1.4 fusion.40
  111.8 1.3 collective-permute-start.4
  113.1 8.0 %collective-permute-start.5 = (f32[24,1,128,128]{3,2,1,0:T(8,128)S(1)}, f32[24,1,128,128]{3,2,1,0:T(8,128)S(1)}, u32[]{:S(2)}, u32[]{:S(2)}) collective-permute-start(f32[24,1,128,128]{3,2,1,0:T(8,128)S(1)} %get-tuple-element.12), channel_id=1, source_target_pairs={{0,1},{1,2},{2,3},{3,4},{4,5},{5,6},{6,7},{7,8},{8,9},{9,10},{10,1... | collective-permute-start | bytes 4718600 | tf_op jit(solution)/shard_map/ppermute | solution.py:24
  121.1 224.5 %collective-permute-done = f32[24,1,128,128]{3,2,1,0:T(8,128)S(1)} collective-permute-done((f32[24,1,128,128]{3,2,1,0:T(8,128)S(1)}, f32[24,1,128,128]{3,2,1,0:T(8,128)S(1)}, u32[]{:S(2)}, u32[]{:S(2)}) %collective-permute-start) | collective-permute-done | bytes 1572896 | tf_op jit(solution)/shard_map/ppermute | solution.py:26
  345.6 2.2 fusion.4
  347.8 0.3 fusion.37
  348.1 1.3 collective-permute-start.2
  349.4 8.0 %collective-permute-start.3 = (f32[24,1,128,128]{3,2,1,0:T(8,128)S(1)}, f32[24,1,128,128]{3,2,1,0:T(8,128)S(1)}, u32[]{:S(2)}, u32[]{:S(2)}) collective-permute-start(f32[24,1,128,128]{3,2,1,0:T(8,128)S(1)} %get-tuple-element.6), channel_id=1, source_target_pairs={{0,1},{1,2},{2,3},{3,4},{4,5},{5,6},{6,7},{7,8},{8,9},{9,10},{10,1... | collective-permute-start | bytes 4718600 | tf_op jit(solution)/shard_map/ppermute | solution.py:24
  357.4 141.8 %collective-permute-done.4 = f32[24,1,128,128]{3,2,1,0:T(8,128)S(1)} collective-permute-done((f32[24,1,128,128]{3,2,1,0:T(8,128)}, f32[24,1,128,128]{3,2,1,0:T(8,128)S(1)}, u32[]{:S(2)}, u32[]{:S(2)}) %collective-permute-start.4) | collective-permute-done | bytes 1572896 | tf_op jit(solution)/shard_map/ppermute | solution.py:26
  499.3 2.2 fusion.14
  501.5 1.4 fusion.39
  502.9 1.3 collective-permute-start.6
  504.2 8.0 %collective-permute-start.7 = (f32[24,1,128,128]{3,2,1,0:T(8,128)S(1)}, f32[24,1,128,128]{3,2,1,0:T(8,128)S(1)}, u32[]{:S(2)}, u32[]{:S(2)}) collective-permute-start(f32[24,1,128,128]{3,2,1,0:T(8,128)S(1)} %get-tuple-element.10), channel_id=1, source_target_pairs={{0,1},{1,2},{2,3},{3,4},{4,5},{5,6},{6,7},{7,8},{8,9},{9,10},{10,1... | collective-permute-start | bytes 4718600 | tf_op jit(solution)/shard_map/ppermute | solution.py:24
  512.2 0.6 fusion.41
  512.9 103.4 %collective-permute-done.2 = f32[24,1,128,128]{3,2,1,0:T(8,128)S(1)} collective-permute-done((f32[24,1,128,128]{3,2,1,0:T(8,128)S(1)}, f32[24,1,128,128]{3,2,1,0:T(8,128)S(1)}, u32[]{:S(2)}, u32[]{:S(2)}) %collective-permute-start.2) | collective-permute-done | bytes 1572896 | tf_op jit(solution)/shard_map/ppermute | solution.py:26
  616.3 2.2 fusion.9
  618.6 36.8 %collective-permute-done.6 = f32[24,1,128,128]{3,2,1,0:T(8,128)S(1)} collective-permute-done((f32[24,1,128,128]{3,2,1,0:T(8,128)}, f32[24,1,128,128]{3,2,1,0:T(8,128)S(1)}, u32[]{:S(2)}, u32[]{:S(2)}) %collective-permute-start.6) | collective-permute-done | bytes 1572896 | tf_op jit(solution)/shard_map/ppermute | solution.py:26
  655.4 2.2 fusion.19
  657.6 4.5 fusion.30
  (10 shorter events, 0.1 us)
Async XLA Ops:
  6.5 46.6 %all-gather.5.cloned.1.call-start = ((), (), s32[]{:S(2)}) async-start(), calls=%async_computation | async-start | bytes 2359296 | tf_op jit(solution)/shard_map/all_gather | solution.py:13
  6.5 91.9 %copy-start = (f32[12,2,128,128]{3,2,1,0:T(8,128)S(1)}, f32[12,2,128,128]{3,2,1,0:T(8,128)}, u32[]{:S(2)}) copy-start(f32[12,2,128,128]{3,2,1,0:T(8,128)} %param.2) | copy-start | bytes 4718596
  8.5 88.1 %all-gather.7.cloned.1.call-start = ((), (), s32[]{:S(2)}) async-start(), calls=%async_computation.1 | async-start | bytes 2359296 | tf_op jit(solution)/shard_map/all_gather | solution.py:13
  101.0 244.5 %collective-permute-start = (f32[24,1,128,128]{3,2,1,0:T(8,128)S(1)}, f32[24,1,128,128]{3,2,1,0:T(8,128)S(1)}, u32[]{:S(2)}, u32[]{:S(2)}) collective-permute-start(f32[24,1,128,128]{3,2,1,0:T(8,128)S(1)} %get-tuple-element.7), channel_id=1, source_target_pairs={{1,0},{2,1},{3,2},{4,3},{5,4},{6,5},{7,6},{8,7},{9,8},{10,9},{11,1... | collective-permute-start | bytes 4718600 | tf_op jit(solution)/shard_map/ppermute | solution.py:26
  102.3 243.2 %collective-permute-start.1 = (f32[24,1,128,128]{3,2,1,0:T(8,128)S(1)}, f32[24,1,128,128]{3,2,1,0:T(8,128)S(1)}, u32[]{:S(2)}, u32[]{:S(2)}) collective-permute-start(f32[24,1,128,128]{3,2,1,0:T(8,128)S(1)} %get-tuple-element.8), channel_id=1, source_target_pairs={{0,1},{1,2},{2,3},{3,4},{4,5},{5,6},{6,7},{7,8},{8,9},{9,10},{10,1... | collective-permute-start | bytes 4718600 | tf_op jit(solution)/shard_map/ppermute | solution.py:24
  111.8 387.5 %collective-permute-start.4 = (f32[24,1,128,128]{3,2,1,0:T(8,128)}, f32[24,1,128,128]{3,2,1,0:T(8,128)S(1)}, u32[]{:S(2)}, u32[]{:S(2)}) collective-permute-start(f32[24,1,128,128]{3,2,1,0:T(8,128)} %get-tuple-element.11), channel_id=1, source_target_pairs={{1,0},{2,1},{3,2},{4,3},{5,4},{6,5},{7,6},{8,7},{9,8},{10,9},{11,1... | collective-permute-start | bytes 4718600 | tf_op jit(solution)/shard_map/ppermute | solution.py:26
  113.1 386.2 %collective-permute-start.5 = (f32[24,1,128,128]{3,2,1,0:T(8,128)S(1)}, f32[24,1,128,128]{3,2,1,0:T(8,128)S(1)}, u32[]{:S(2)}, u32[]{:S(2)}) collective-permute-start(f32[24,1,128,128]{3,2,1,0:T(8,128)S(1)} %get-tuple-element.12), channel_id=1, source_target_pairs={{0,1},{1,2},{2,3},{3,4},{4,5},{5,6},{6,7},{7,8},{8,9},{9,10},{10,1... | collective-permute-start | bytes 4718600 | tf_op jit(solution)/shard_map/ppermute | solution.py:24
  348.1 268.2 %collective-permute-start.2 = (f32[24,1,128,128]{3,2,1,0:T(8,128)S(1)}, f32[24,1,128,128]{3,2,1,0:T(8,128)S(1)}, u32[]{:S(2)}, u32[]{:S(2)}) collective-permute-start(f32[24,1,128,128]{3,2,1,0:T(8,128)S(1)} %get-tuple-element.5), channel_id=1, source_target_pairs={{1,0},{2,1},{3,2},{4,3},{5,4},{6,5},{7,6},{8,7},{9,8},{10,9},{11,1... | collective-permute-start | bytes 4718600 | tf_op jit(solution)/shard_map/ppermute | solution.py:26
  349.4 266.9 %collective-permute-start.3 = (f32[24,1,128,128]{3,2,1,0:T(8,128)S(1)}, f32[24,1,128,128]{3,2,1,0:T(8,128)S(1)}, u32[]{:S(2)}, u32[]{:S(2)}) collective-permute-start(f32[24,1,128,128]{3,2,1,0:T(8,128)S(1)} %get-tuple-element.6), channel_id=1, source_target_pairs={{0,1},{1,2},{2,3},{3,4},{4,5},{5,6},{6,7},{7,8},{8,9},{9,10},{10,1... | collective-permute-start | bytes 4718600 | tf_op jit(solution)/shard_map/ppermute | solution.py:24
  501.5 10.7 %copy-start.1 = (f32[96]{0:T(128)S(1)}, f32[96]{0:T(128)}, u32[]{:S(2)}) copy-start(f32[96]{0:T(128)} %param.3) | copy-start | bytes 1156
  502.9 152.4 %collective-permute-start.6 = (f32[24,1,128,128]{3,2,1,0:T(8,128)}, f32[24,1,128,128]{3,2,1,0:T(8,128)S(1)}, u32[]{:S(2)}, u32[]{:S(2)}) collective-permute-start(f32[24,1,128,128]{3,2,1,0:T(8,128)} %get-tuple-element.9), channel_id=1, source_target_pairs={{1,0},{2,1},{3,2},{4,3},{5,4},{6,5},{7,6},{8,7},{9,8},{10,9},{11,1... | collective-permute-start | bytes 4718600 | tf_op jit(solution)/shard_map/ppermute | solution.py:26
  504.2 151.2 %collective-permute-start.7 = (f32[24,1,128,128]{3,2,1,0:T(8,128)S(1)}, f32[24,1,128,128]{3,2,1,0:T(8,128)S(1)}, u32[]{:S(2)}, u32[]{:S(2)}) collective-permute-start(f32[24,1,128,128]{3,2,1,0:T(8,128)S(1)} %get-tuple-element.10), channel_id=1, source_target_pairs={{0,1},{1,2},{2,3},{3,4},{4,5},{5,6},{6,7},{7,8},{8,9},{9,10},{10,1... | collective-permute-start | bytes 4718600 | tf_op jit(solution)/shard_map/ppermute | solution.py:24
Sparse Core Ops, SparseCore 0:
  9.4 43.6 all-gather.4
  55.2 41.4 all-gather.6
